TPU v7x, 256 devices: a whole 4x4x8 slice. The times are simulated.
256 devices in a mesh: ctx: 64 (over x_lo, y, z), kvh: 4 (over x_hi, core).
Axes of the slice: x: 4 (x_hi: 2, x_lo: 2; x = x_hi * 2 + x_lo), y: 4, z: 8, core: 2. Of those that a mesh axis runs over, the one named last changes fastest.
Arguments:
- queries: bfloat16 [16384, 2048], P(('ctx', 'kvh')), may hold values from -42 to 42
- keys: bfloat16 [16384, 512], P(('ctx', 'kvh')), may hold values from -6 to 6
- values: bfloat16 [16384, 512], P(('ctx', 'kvh')), may hold values from -6 to 6
- doc_lengths: int32 [16], replicated, may hold values from 1 to 8192, 16384 in all
Outputs:
- attended: bfloat16 [16384, 2048], P(('ctx', 'kvh'))
Inputs may be any that keep to these rules, and one draw needn't show every extreme that they name: `doc_lengths`: positive lengths that sum to 16384.
All inputs are finite; a program needn't handle non-finite values.
Results may differ from a plain program's by a relative error of at most 0.005.
Values may be sent and summed in bfloat16 or wider, within the bound.
No kernel may reach another device: no remote copies, remote signals or barrier semaphores. Data moves between devices by JAX's collectives and lax.ppermute only.
A program may use at most 64 MiB of HBM per device.

v0:
```python
import functools

import jax
import jax.numpy as jnp
from jax import lax
from jax.experimental import pallas as pl
from jax.experimental.pallas import tpu as pltpu
from jax.sharding import Mesh
from jax.sharding import PartitionSpec as P

HEAD = 128
SINK = 128
GROUP = ("ctx_0", "ctx_1")
RING = "ctx_2"
CTX_KVH = ("ctx_0", "ctx_1", "ctx_2", "kvh")
N_GROUPS, N_RING = 8, 8
REACH = 4
BLOCK = 256
GROUP_KEYS = N_RING * BLOCK
HALF = GROUP_KEYS // 2
UNROLL = 4
NEG = -1e30
LOG2E = 1.4426950408889634
SCALE = HEAD**-0.5 * LOG2E


LOW, HIGH, TINY = 2.0**-96, 2.0**96, 2.0**-120
LANES = 128
GATE = 24
NT = (((1,), (1,)), ((), ()))


def document_bounds(meta_ref):
    lane = lax.broadcasted_iota(jnp.int32, (1, LANES), 1)
    first, end = jnp.zeros((1, LANES), jnp.int32), jnp.zeros((1, LANES), jnp.int32)
    at = jnp.int32(0)
    for i in range(16):
        first = jnp.where(lane == i, at, first)
        at = at + meta_ref[2 + i]
        end = jnp.where(lane == i, at, end)
    return first, end


def start_of(meta_ref, pos):
    start, at = jnp.zeros_like(pos), jnp.int32(0)
    for i in range(15):
        at = at + meta_ref[2 + i]
        start = jnp.where(pos >= at, at, start)
    return start


def assemble(meta_ref, *refs):
    blocks, (k_ref, v_ref) = refs[:9], refs[9:]
    g, z = meta_ref[0], meta_ref[1]
    first, end = document_bounds(meta_ref)
    half = BLOCK // 2
    pieces = [(r, 0, ref) for ref, r in zip(blocks[:7], (0, 1, 7, 2, 6, 3, 5))]
    pieces += [(4, 0, blocks[7]), (4, half, blocks[8])]
    for r, offset, ref in pieces:
        n = ref.shape[0]
        block = lax.rem(z - r + N_RING, N_RING)
        at = pl.multiple_of(block * BLOCK + offset, half)
        rows = pl.ds(at, n)
        pos = g * GROUP_KEYS + at + lax.broadcasted_iota(jnp.int32, (n, 1), 0)
        seen = ((pos >= first) & (pos < end)) | (pos < SINK)
        k_ref[rows, :HEAD] = ref[:, :HEAD]
        k_ref[rows, HEAD:] = jnp.where(seen, 0.0, NEG).astype(k_ref.dtype)
        v_ref[rows, :HEAD] = ref[:, HEAD:]
        v_ref[rows, HEAD:] = jnp.ones((n, HEAD), v_ref.dtype)


def query_columns(meta_ref, q_first):
    first, end = document_bounds(meta_ref)
    pos = q_first + lax.broadcasted_iota(jnp.int32, (BLOCK, 1), 0)
    return jnp.where((pos >= first) & (pos < end), 1.0, 0.0).astype(jnp.bfloat16)


def scores(q, k):
    return lax.dot_general(q, k, NT, preferred_element_type=jnp.float32)


def finish(out_ref, stats_ref, h, o, m=None):
    total = o[:, HEAD:]
    cols = pl.ds(pl.multiple_of(h * HEAD, HEAD), HEAD)
    out_ref[:BLOCK, cols] = (o[:, :HEAD] / jnp.maximum(total, TINY)).astype(out_ref.dtype)
    lane = lax.broadcasted_iota(jnp.int32, total.shape, 1)
    stats = jnp.where(lane == h, total, stats_ref[...])
    stats_ref[...] = stats if m is None else jnp.where(lane == 8 + h, m, stats)


def put_stats(out_ref, rows, m):
    lse = (0.0 if m is None else m) + jnp.where(rows > 0.0, jnp.log2(jnp.maximum(rows, TINY)), NEG)
    words = []
    for _ in range(3):
        word = lse.astype(jnp.bfloat16).astype(jnp.float32)
        words.append(word)
        lse = lse - word
    lower = jnp.concatenate([words[0][:4], words[1][:4]], axis=0)
    out_ref[BLOCK:, :BLOCK] = jnp.concatenate([lower, words[2]], axis=0).astype(out_ref.dtype)
    out_ref[BLOCK:, BLOCK:] = jnp.zeros((16, out_ref.shape[1] - BLOCK), out_ref.dtype)


def weights_of(s, m=None):
    return jnp.exp2((s if m is None else s - m) * SCALE).astype(jnp.bfloat16)


def product(p, v):
    return jnp.dot(p, v, preferred_element_type=jnp.float32)


def attend(d, meta_ref, q_ref, k_ref, v_ref, *refs):
    own = d == 0
    sink_refs, (out_ref, acc_ref, p_ref, stats_ref, mask_ref) = refs[: int(own)], refs[int(own) :]
    heads = q_ref.shape[1] // HEAD
    g, z = meta_ref[0], meta_ref[1]
    q_first = (g + d) * GROUP_KEYS + z * BLOCK
    key_first, key_end = g * GROUP_KEYS, (g + 1) * GROUP_KEYS
    reach = start_of(meta_ref, q_first)
    far = g > REACH

    def query(h):
        return jnp.concatenate([q_ref[:, pl.ds(pl.multiple_of(h * HEAD, HEAD), HEAD)], mask_ref[...]], axis=1)

    def seen_scores(q, at):
        s = scores(q, k_ref[pl.ds(pl.multiple_of(at, BLOCK), BLOCK), :])
        if not own:
            return s
        row = lax.broadcasted_iota(jnp.int32, (BLOCK, BLOCK), 0)
        column = lax.broadcasted_iota(jnp.int32, (BLOCK, BLOCK), 1)
        return jnp.where(column - row <= z * BLOCK - at, s, NEG)

    def sink_scores(q):
        return scores(q[:, :HEAD], sink_refs[0][:, :HEAD])

    def sink_values():
        return jnp.concatenate([sink_refs[0][:, HEAD:], jnp.ones((SINK, HEAD), jnp.bfloat16)], axis=1)

    def each_head(body):
        lax.fori_loop(0, heads, lambda h, _: (body(h), 0)[1], 0)

    def store():
        stats_ref[...] = jnp.zeros((BLOCK, LANES), jnp.float32)
        for h in range(heads):
            finish(out_ref, stats_ref, h, acc_ref[h])
        totals = stats_ref[...].T[:8]
        put_stats(out_ref, totals, None)
        head = lax.broadcasted_iota(jnp.int32, totals.shape, 0)
        visible = head < heads
        if not own:
            pos = q_first + lax.broadcasted_iota(jnp.int32, totals.shape, 1)
            visible = visible & ((start_of(meta_ref, pos) < key_end) | (g == 0))
        off = visible & jnp.logical_not((totals >= LOW) & (totals <= HIGH))

        @pl.when(jnp.max(jnp.where(off, 1.0, 0.0)) > 0.0)
        def _():
            each_head(careful)
            rows = stats_ref[...].T
            put_stats(out_ref, rows[:8], rows[8:16])

    def careful(h):
        q = query(h)
        m = lax.fori_loop(
            0,
            N_RING,
            lambda r, m: jnp.maximum(m, jnp.max(seen_scores(q, r * BLOCK), axis=1, keepdims=True)),
            jnp.full((BLOCK, 1), 2 * NEG, jnp.float32),
        )
        if own:
            m = jnp.where(far, jnp.maximum(m, jnp.max(sink_scores(q), axis=1, keepdims=True)), m)

        def add(r, o):
            v = v_ref[pl.ds(pl.multiple_of(r * BLOCK, BLOCK), BLOCK), :]
            return o + product(weights_of(seen_scores(q, r * BLOCK), m), v)

        o = lax.fori_loop(0, N_RING, add, jnp.zeros((BLOCK, 2 * HEAD), jnp.float32))
        if own:
            o = o + jnp.where(far, product(weights_of(sink_scores(q), m), sink_values()), 0.0)
        finish(out_ref, stats_ref, h, o, m * SCALE)

    def over_halves():
        acc_ref[...] = jnp.zeros(acc_ref.shape, jnp.float32)
        low = ((reach >= key_first + HALF) & (g > 0)).astype(jnp.int32)
        high = 1 + (z * BLOCK >= HALF).astype(jnp.int32) if own else 2
        turns = heads // UNROLL

        def step(i, _):
            at = lax.div(i, turns) * HALF
            for u in range(UNROLL):
                h = lax.rem(i, turns) * UNROLL + u
                q = query(h)
                for r in range(0, HALF, BLOCK):
                    p_ref[u, :, r : r + BLOCK] = weights_of(seen_scores(q, at + r))
                acc_ref[h] += product(p_ref[u], v_ref[pl.ds(pl.multiple_of(at, HALF), HALF), :])
            return 0

        lax.fori_loop(low * turns, high * turns, step, 0)

    if own:
        mask_ref[...] = query_columns(meta_ref, q_first)
        over_halves()

        @pl.when(far)
        def _():
            def add_sink(h):
                acc_ref[h] += product(weights_of(sink_scores(query(h))), sink_values())

            each_head(add_sink)

        store()
        return
    near = reach < key_end
    active = (g + d < N_GROUPS) & (near | (g == 0))

    @pl.when(active)
    def _():
        mask_ref[...] = query_columns(meta_ref, q_first)
        pl.when(near)(over_halves)

        @pl.when(jnp.logical_not(near))
        def _():
            def only_sink(h):
                acc_ref[h] = product(weights_of(seen_scores(query(h), 0)), v_ref[:BLOCK, :])

            each_head(only_sink)

        store()

    @pl.when(jnp.logical_not(active))
    def _():
        out_ref[:BLOCK, :] = jnp.zeros((BLOCK, q_ref.shape[1]), out_ref.dtype)
        out_ref[BLOCK:, :] = jnp.full((16, q_ref.shape[1]), NEG, out_ref.dtype)


def merge(meta_ref, own_ref, *refs):
    parts, out_ref = refs[:REACH], refs[REACH]
    g = meta_ref[0]
    heads = out_ref.shape[1] // HEAD

    def lse_of(ref):
        words = ref[BLOCK:, :BLOCK].astype(jnp.float32)
        return words[0:4] + words[4:8] + words[8:12]

    lses = [lse_of(own_ref)] + [jnp.where(g >= d, lse_of(ref), NEG) for d, ref in enumerate(parts, 1)]
    top = functools.reduce(jnp.maximum, lses)
    weights = [jnp.exp2(x - top) for x in lses]
    total = functools.reduce(jnp.add, weights)
    rows = [w / total for w in weights]
    rows.append(jnp.zeros((LANES - heads * (REACH + 1), BLOCK), jnp.float32))
    columns = jnp.concatenate(rows, axis=0).T
    for h in range(heads):
        cols = slice(h * HEAD, (h + 1) * HEAD)
        acc = own_ref[:BLOCK, cols] * columns[:, h : h + 1]
        for d, ref in enumerate(parts, 1):
            acc = acc + ref[:BLOCK, cols].astype(jnp.float32) * columns[:, heads * d + h : heads * d + h + 1]
        out_ref[:, cols] = acc.astype(out_ref.dtype)


VMEM = pl.BlockSpec(memory_space=pltpu.VMEM)
SMEM = pl.BlockSpec(memory_space=pltpu.SMEM)


def assemble_call(meta, blocks):
    return pl.pallas_call(
        assemble,
        name="assemble",
        out_shape=[jax.ShapeDtypeStruct((GROUP_KEYS, 2 * HEAD), jnp.bfloat16)] * 2,
        in_specs=[SMEM] + [VMEM] * len(blocks),
        out_specs=[VMEM, VMEM],
        compiler_params=pltpu.CompilerParams(vmem_limit_bytes=12 << 20),
        cost_estimate=pl.CostEstimate(flops=1 << 20, transcendentals=0, bytes_accessed=3 << 20),
    )(meta, *blocks)


def cost(width):
    return pl.CostEstimate(flops=2 * BLOCK * GROUP_KEYS * width, transcendentals=0, bytes_accessed=3 << 20)


def attend_call(d, meta, q, k, v, *sink):
    width = q.shape[1]
    return pl.pallas_call(
        functools.partial(attend, d),
        name=f"attend_{d}",
        out_shape=jax.ShapeDtypeStruct((BLOCK + 16, width), jnp.bfloat16 if d else jnp.float32),
        in_specs=[SMEM] + [VMEM] * (3 + len(sink)),
        out_specs=VMEM,
        scratch_shapes=[
            pltpu.VMEM((width // HEAD, BLOCK, 2 * HEAD), jnp.float32),
            pltpu.VMEM((UNROLL, BLOCK, HALF), jnp.bfloat16),
            pltpu.VMEM((BLOCK, LANES), jnp.float32),
            pltpu.VMEM((BLOCK, LANES), jnp.bfloat16),
        ],
        compiler_params=pltpu.CompilerParams(vmem_limit_bytes=20 << 20),
        cost_estimate=cost(width),
    )(meta, q, k, v, *sink)


def merge_call(meta, own, parts):
    return pl.pallas_call(
        merge,
        name="merge",
        out_shape=jax.ShapeDtypeStruct((BLOCK, own.shape[1]), jnp.bfloat16),
        in_specs=[SMEM] + [VMEM] * (1 + len(parts)),
        out_specs=VMEM,
        compiler_params=pltpu.CompilerParams(vmem_limit_bytes=16 << 20),
    )(meta, own, *parts)


def along_ring(x, step):
    return lax.ppermute(x, RING, [(i, (i + step) % N_RING) for i in range(N_RING)])


def to_group(x, step):
    return lax.ppermute(x, GROUP, [(i, i + step) for i in range(N_GROUPS) if 0 <= i + step < N_GROUPS])


def shards(queries, keys, values, doc_lengths):
    rows = queries.shape[0]
    kv_heads = keys.shape[1] // HEAD
    by_head = jnp.concatenate([x.reshape(rows, kv_heads, -1) for x in (queries, keys, values)], axis=2)
    mine = lax.all_to_all(by_head.reshape(rows, -1), "kvh", split_axis=1, concat_axis=0, tiled=True)
    width = queries.shape[1] // kv_heads
    q, kv = mine[:, :width], mine[:, width:]
    g, z = lax.axis_index(GROUP), lax.axis_index(RING)
    meta = jnp.concatenate([jnp.stack([g, z]).astype(jnp.int32), doc_lengths])

    half = BLOCK // 2
    visiting = {}
    blocks, up, down = [kv], kv, kv
    for step in range(3):
        up, down = along_ring(up, 1), along_ring(down, -1)
        visiting[REACH - step] = to_group(q, step - REACH)
        blocks += [up, down]
    blocks += [along_ring(up[:half], 1), along_ring(down[half:], -1)]
    visiting[1] = to_group(q, -1)

    k, v = assemble_call(meta, blocks)
    parts = {}
    first = blocks[0][:half]
    for r, i in enumerate((1, 3, 5, 7, 6, 4, 2), 1):
        first = jnp.where(z == r, blocks[i][:half], first)
    order = (1, 2, 3, 4)
    for turn, d in enumerate(order):
        part = attend_call(d, meta, visiting[d], k, v)
        if turn == 1:
            part, first = lax.optimization_barrier((part, first))
            sink = jnp.zeros_like(first)
            for far in range(REACH + 1, N_GROUPS):
                sink = jnp.where(g == far, lax.ppermute(first, GROUP, [(0, far)]), sink)
        parts[d] = to_group(part, d)
    own = attend_call(0, meta, q, k, v, sink)
    parts = [parts[d] for d in range(1, REACH + 1)]
    out = merge_call(meta, own, parts)
    return lax.all_to_all(out, "kvh", split_axis=0, concat_axis=1, tiled=True)


def solution(mesh):
    torus = Mesh(mesh.devices.reshape(2, 4, 8, mesh.shape["kvh"]), CTX_KVH)
    in_specs = (P(CTX_KVH, None), P(CTX_KVH, None), P(CTX_KVH, None), P())
    return jax.shard_map(
        shards, mesh=torus, in_specs=in_specs, out_specs=P(CTX_KVH, None), check_vma=False
    )
```

profile of v0, /device:TPU:1, one launch (start us, length us, event | category | flops | bytes accessed | tf_op | source)
XLA Modules:
  0.0 210.9 jit_solution(14096354083921174258)
XLA Ops:
  1.1 13.5 %all_to_all.35 = bf16[64,4,768]{2,0,1:T(8,128)(2,1)S(1)} all-to-all(bf16[64,4,768]{2,0,1:T(8,128)(2,1)S(1)} %pad_maximum_fusion), channel_id=1, replica_groups=mesh['ctx_0'=2,'ctx_1'=4,'ctx_2'=8,'kvh'=4] {'kvh'}, dimensions={1} | all-to-all | bytes 786432 | tf_op jit(solution)/shard_map/all_to_all | solution.py:320
  14.7 1.7 collective-permute-start
  16.3 4.0 %collective-permute-start.1 = (bf16[256,256]{1,0:T(8,128)(2,1)S(1)}, bf16[256,256]{1,0:T(8,128)(2,1)S(1)}, u32[]{:S(2)}, u32[]{:S(2)}) collective-permute-start(bf16[256,256]{1,0:T(8,128)(2,1)S(1)} %slice.43.refs_0_), channel_id=1, source_target_pairs={{0,28},{4,0},{8,4},{12,8},{16,12},{20,16},{24,20},{28,24},{1,29},{... | collective-permute-start | bytes 393224 | tf_op jit(solution)/shard_map/ppermute | solution.py:309
  20.4 2.7 %collective-permute-done.refs_1_ = bf16[256,256]{1,0:T(8,128)(2,1)S(1)} collective-permute-done((bf16[256,256]{1,0:T(8,128)(2,1)S(1)}, bf16[256,256]{1,0:T(8,128)(2,1)S(1)}, u32[]{:S(2)}, u32[]{:S(2)}) %collective-permute-start) | collective-permute-done | bytes 131104 | tf_op jit(solution)/shard_map/ppermute | solution.py:309
  23.1 2.7 %collective-permute-start.3 = (bf16[256,256]{1,0:T(8,128)(2,1)S(1)}, bf16[256,256]{1,0:T(8,128)(2,1)S(1)}, u32[]{:S(2)}, u32[]{:S(2)}) collective-permute-start(bf16[256,256]{1,0:T(8,128)(2,1)S(1)} %collective-permute-done.1.refs_2_), channel_id=1, source_target_pairs={{0,28},{4,0},{8,4},{12,8},{16,12},{20,16},{24,20},{28,24},{1,29},{... | collective-permute-start | bytes 393224 | tf_op jit(solution)/shard_map/ppermute | solution.py:309
  25.8 2.3 %collective-permute-done.2.refs_3_ = bf16[256,256]{1,0:T(8,128)(2,1)S(1)} collective-permute-done((bf16[256,256]{1,0:T(8,128)(2,1)S(1)}, bf16[256,256]{1,0:T(8,128)(2,1)S(1)}, u32[]{:S(2)}, u32[]{:S(2)}) %collective-permute-start.2) | collective-permute-done | bytes 131104 | tf_op jit(solution)/shard_map/ppermute | solution.py:309
  28.1 2.7 %collective-permute-start.5 = (bf16[256,256]{1,0:T(8,128)(2,1)S(1)}, bf16[256,256]{1,0:T(8,128)(2,1)S(1)}, u32[]{:S(2)}, u32[]{:S(2)}) collective-permute-start(bf16[256,256]{1,0:T(8,128)(2,1)S(1)} %collective-permute-done.3.refs_4_), channel_id=1, source_target_pairs={{0,28},{4,0},{8,4},{12,8},{16,12},{20,16},{24,20},{28,24},{1,29},{... | collective-permute-start | bytes 393224 | tf_op jit(solution)/shard_map/ppermute | solution.py:309
  30.8 2.3 %collective-permute-done.4.refs_5_ = bf16[256,256]{1,0:T(8,128)(2,1)S(1)} collective-permute-done((bf16[256,256]{1,0:T(8,128)(2,1)S(1)}, bf16[256,256]{1,0:T(8,128)(2,1)S(1)}, u32[]{:S(2)}, u32[]{:S(2)}) %collective-permute-start.4) | collective-permute-done | bytes 131104 | tf_op jit(solution)/shard_map/ppermute | solution.py:309
  37.1 1.3 collective-permute-start.17
  38.5 2.7 %collective-permute-start.7 = (bf16[128,256]{1,0:T(8,128)(2,1)S(1)}, bf16[128,256]{1,0:T(8,128)(2,1)S(1)}, u32[]{:S(2)}, u32[]{:S(2)}) collective-permute-start(bf16[128,256]{1,0:T(8,128)(2,1)S(1)} %get-tuple-element.14), channel_id=1, source_target_pairs={{0,28},{4,0},{8,4},{12,8},{16,12},{20,16},{24,20},{28,24},{1,29},{... | collective-permute-start | bytes 196616 | tf_op jit(solution)/shard_map/ppermute | solution.py:309
  43.7 24.8 %attend_2.1 = bf16[272,512]{1,0:T(8,128)(2,1)S(1)} custom-call(s32[18]{0:T(128)S(1)} %pad_add_fusion.meta_ref, bf16[256,512]{1,0:T(8,128)(2,1)S(1)} %collective-permute-done.8.q_ref, bf16[2048,256]{1,0:T(8,128)(2,1)S(1)} %get-tuple-element.9.k_ref, bf16[2048,256]{1,0:T(8,128)(2,1)S(1)} %get-tuple-element.10.v_ref), custom_call_target="tpu_custom_call" | custom-call | flops 536870912 | bytes 3145728 | tf_op jit(solution)/shard_map/attend_2/pallas_call | solution.py:280
  68.5 1.3 collective-permute-start.9
  69.8 1.3 collective-permute-start.10
  71.1 8.6 %collective-permute-start.11 = (bf16[128,256]{1,0:T(8,128)(2,1)S(1)}, bf16[128,256]{1,0:T(8,128)(2,1)S(1)}, u32[]{:S(2)}, u32[]{:S(2)}) collective-permute-start(bf16[128,256]{1,0:T(8,128)(2,1)S(1)} %get-tuple-element.11), channel_id=1, source_target_pairs={{0,160},{1,161},{2,162},{3,163},{4,164},{5,165},{6,166},{7,167},{8... | collective-permute-start | bytes 196616 | tf_op jit(solution)/shard_map/ppermute | solution.py:348
  79.7 26.2 %attend_1.1 = bf16[272,512]{1,0:T(8,128)(2,1)S(1)} custom-call(s32[18]{0:T(128)S(1)} %pad_add_fusion.meta_ref, bf16[256,512]{1,0:T(8,128)(2,1)S(1)} %collective-permute-done.12.q_ref, bf16[2048,256]{1,0:T(8,128)(2,1)S(1)} %get-tuple-element.9.k_ref, bf16[2048,256]{1,0:T(8,128)(2,1)S(1)} %get-tuple-element.10.v_ref), custom_call_target="tpu_custom_call" | custom-call | flops 536870912 | bytes 3145728 | tf_op jit(solution)/shard_map/attend_1/pallas_call | solution.py:280
  105.9 1.5 collective-permute-start.13
  107.4 2.4 %attend_3.1 = bf16[272,512]{1,0:T(8,128)(2,1)S(1)} custom-call(s32[18]{0:T(128)S(1)} %pad_add_fusion.meta_ref, bf16[256,512]{1,0:T(8,128)(2,1)S(1)} %collective-permute-done.15.q_ref, bf16[2048,256]{1,0:T(8,128)(2,1)S(1)} %get-tuple-element.9.k_ref, bf16[2048,256]{1,0:T(8,128)(2,1)S(1)} %get-tuple-element.10.v_ref), custom_call_target="tpu_custom_call" | custom-call | flops 536870912 | bytes 3145728 | tf_op jit(solution)/shard_map/attend_3/pallas_call | solution.py:280
  109.8 1.3 collective-permute-start.14
  111.1 2.4 %attend_4.1 = bf16[272,512]{1,0:T(8,128)(2,1)S(1)} custom-call(s32[18]{0:T(128)S(1)} %pad_add_fusion.meta_ref, bf16[256,512]{1,0:T(8,128)(2,1)S(1)} %collective-permute-done.17.q_ref, bf16[2048,256]{1,0:T(8,128)(2,1)S(1)} %get-tuple-element.9.k_ref, bf16[2048,256]{1,0:T(8,128)(2,1)S(1)} %get-tuple-element.10.v_ref), custom_call_target="tpu_custom_call" | custom-call | flops 536870912 | bytes 3145728 | tf_op jit(solution)/shard_map/attend_4/pallas_call | solution.py:280
  113.5 52.2 %collective-permute-start.16 = (bf16[272,512]{1,0:T(8,128)(2,1)S(1)}, bf16[272,512]{1,0:T(8,128)(2,1)S(1)}, u32[]{:S(2)}, u32[]{:S(2)}) collective-permute-start(bf16[272,512]{1,0:T(8,128)(2,1)S(1)} %attend_3.1), channel_id=1, source_target_pairs={{0,96},{32,128},{64,160},{96,192},{128,224},{1,97},{33,129},{65,16... | collective-permute-start | bytes 835592 | tf_op jit(solution)/shard_map/ppermute | solution.py:313
  165.7 1.3 collective-permute-start.18
  167.1 26.5 %attend_0.1.own_ref = f32[272,512]{1,0:T(8,128)S(1)} custom-call(s32[18]{0:T(128)S(1)} %pad_add_fusion.meta_ref, bf16[256,512]{1,0:T(8,128)(2,1)S(1)} %slice.42.q_ref, bf16[2048,256]{1,0:T(8,128)(2,1)S(1)} %get-tuple-element.9.k_ref, bf16[2048,256]{1,0:T(8,128)(2,1)S(1)} %get-tuple-element.10.v_ref, bf16[128,256]{1,0:T(8,128)(2,1)S(1)} %select_select_fusion.refs_0_), custom_call_target="tpu_custom_call" | custom-call | flops 536870912 | bytes 3145728 | tf_op jit(solution)/shard_map/attend_0/pallas_call | solution.py:280
  193.6 1.5 merge.1
  195.1 15.1 %all_to_all.36 = bf16[4,64,512]{2,1,0:T(8,128)(2,1)S(1)} all-to-all(bf16[4,64,512]{2,1,0:T(8,128)(2,1)S(1)} %bitcast.23), channel_id=1, replica_groups=mesh['ctx_0'=2,'ctx_1'=4,'ctx_2'=8,'kvh'=4] {'kvh'}, dimensions={0} | all-to-all | bytes 524288 | tf_op jit(solution)/shard_map/all_to_all | solution.py:353
  (39 shorter events, 8.3 us)
Async XLA Ops:
  0.0 1.0 copy-start
  0.0 1.0 copy-start.1
  14.7 8.4 %collective-permute-start = (bf16[256,256]{1,0:T(8,128)(2,1)S(1)}, bf16[256,256]{1,0:T(8,128)(2,1)S(1)}, u32[]{:S(2)}, u32[]{:S(2)}) collective-permute-start(bf16[256,256]{1,0:T(8,128)(2,1)S(1)} %slice.43.refs_0_), channel_id=1, source_target_pairs={{0,4},{4,8},{8,12},{12,16},{16,20},{20,24},{24,28},{28,0},{1,5},{5... | collective-permute-start | bytes 393224 | tf_op jit(solution)/shard_map/ppermute | solution.py:309
  16.3 6.8 %collective-permute-start.1 = (bf16[256,256]{1,0:T(8,128)(2,1)S(1)}, bf16[256,256]{1,0:T(8,128)(2,1)S(1)}, u32[]{:S(2)}, u32[]{:S(2)}) collective-permute-start(bf16[256,256]{1,0:T(8,128)(2,1)S(1)} %slice.43.refs_0_), channel_id=1, source_target_pairs={{0,28},{4,0},{8,4},{12,8},{16,12},{20,16},{24,20},{28,24},{1,29},{... | collective-permute-start | bytes 393224 | tf_op jit(solution)/shard_map/ppermute | solution.py:309
  23.1 5.0 %collective-permute-start.2 = (bf16[256,256]{1,0:T(8,128)(2,1)S(1)}, bf16[256,256]{1,0:T(8,128)(2,1)S(1)}, u32[]{:S(2)}, u32[]{:S(2)}) collective-permute-start(bf16[256,256]{1,0:T(8,128)(2,1)S(1)} %collective-permute-done.refs_1_), channel_id=1, source_target_pairs={{0,4},{4,8},{8,12},{12,16},{16,20},{20,24},{24,28},{28,0},{1,5},{5... | collective-permute-start | bytes 393224 | tf_op jit(solution)/shard_map/ppermute | solution.py:309
  23.1 5.0 %collective-permute-start.3 = (bf16[256,256]{1,0:T(8,128)(2,1)S(1)}, bf16[256,256]{1,0:T(8,128)(2,1)S(1)}, u32[]{:S(2)}, u32[]{:S(2)}) collective-permute-start(bf16[256,256]{1,0:T(8,128)(2,1)S(1)} %collective-permute-done.1.refs_2_), channel_id=1, source_target_pairs={{0,28},{4,0},{8,4},{12,8},{16,12},{20,16},{24,20},{28,24},{1,29},{... | collective-permute-start | bytes 393224 | tf_op jit(solution)/shard_map/ppermute | solution.py:309
  28.1 5.0 %collective-permute-start.4 = (bf16[256,256]{1,0:T(8,128)(2,1)S(1)}, bf16[256,256]{1,0:T(8,128)(2,1)S(1)}, u32[]{:S(2)}, u32[]{:S(2)}) collective-permute-start(bf16[256,256]{1,0:T(8,128)(2,1)S(1)} %collective-permute-done.2.refs_3_), channel_id=1, source_target_pairs={{0,4},{4,8},{8,12},{12,16},{16,20},{20,24},{24,28},{28,0},{1,5},{5... | collective-permute-start | bytes 393224 | tf_op jit(solution)/shard_map/ppermute | solution.py:309
  28.1 9.0 %collective-permute-start.5 = (bf16[256,256]{1,0:T(8,128)(2,1)S(1)}, bf16[256,256]{1,0:T(8,128)(2,1)S(1)}, u32[]{:S(2)}, u32[]{:S(2)}) collective-permute-start(bf16[256,256]{1,0:T(8,128)(2,1)S(1)} %collective-permute-done.3.refs_4_), channel_id=1, source_target_pairs={{0,28},{4,0},{8,4},{12,8},{16,12},{20,16},{24,20},{28,24},{1,29},{... | collective-permute-start | bytes 393224 | tf_op jit(solution)/shard_map/ppermute | solution.py:309
  33.1 5.3 %collective-permute-start.6 = (bf16[128,256]{1,0:T(8,128)(2,1)S(1)}, bf16[128,256]{1,0:T(8,128)(2,1)S(1)}, u32[]{:S(2)}, u32[]{:S(2)}) collective-permute-start(bf16[128,256]{1,0:T(8,128)(2,1)S(1)} %slice.44), channel_id=1, source_target_pairs={{0,4},{4,8},{8,12},{12,16},{16,20},{20,24},{24,28},{28,0},{1,5},{5... | collective-permute-start | bytes 196616 | tf_op jit(solution)/shard_map/ppermute | solution.py:309
  33.2 10.5 %collective-permute-start.8 = (bf16[256,512]{1,0:T(8,128)(2,1)S(1)}, bf16[256,512]{1,0:T(8,128)(2,1)S(1)}, u32[]{:S(2)}, u32[]{:S(2)}) collective-permute-start(bf16[256,512]{1,0:T(8,128)(2,1)S(1)} %slice.42.q_ref), channel_id=1, source_target_pairs={{64,0},{96,32},{128,64},{160,96},{192,128},{224,160},{65,1},{97,33... | collective-permute-start | bytes 786440 | tf_op jit(solution)/shard_map/ppermute | solution.py:313
  34.5 36.6 %collective-permute-start.12 = (bf16[256,512]{1,0:T(8,128)(2,1)S(1)}, bf16[256,512]{1,0:T(8,128)(2,1)S(1)}, u32[]{:S(2)}, u32[]{:S(2)}) collective-permute-start(bf16[256,512]{1,0:T(8,128)(2,1)S(1)} %slice.42.q_ref), channel_id=1, source_target_pairs={{32,0},{64,32},{96,64},{128,96},{160,128},{192,160},{224,192},{33,... | collective-permute-start | bytes 786440 | tf_op jit(solution)/shard_map/ppermute | solution.py:313
  35.8 70.1 %collective-permute-start.15 = (bf16[256,512]{1,0:T(8,128)(2,1)S(1)}, bf16[256,512]{1,0:T(8,128)(2,1)S(1)}, u32[]{:S(2)}, u32[]{:S(2)}) collective-permute-start(bf16[256,512]{1,0:T(8,128)(2,1)S(1)} %slice.42.q_ref), channel_id=1, source_target_pairs={{96,0},{128,32},{160,64},{192,96},{224,128},{97,1},{129,33},{161,6... | collective-permute-start | bytes 786440 | tf_op jit(solution)/shard_map/ppermute | solution.py:313
  37.1 72.7 %collective-permute-start.17 = (bf16[256,512]{1,0:T(8,128)(2,1)S(1)}, bf16[256,512]{1,0:T(8,128)(2,1)S(1)}, u32[]{:S(2)}, u32[]{:S(2)}) collective-permute-start(bf16[256,512]{1,0:T(8,128)(2,1)S(1)} %slice.42.q_ref), channel_id=1, source_target_pairs={{128,0},{160,32},{192,64},{224,96},{129,1},{161,33},{193,65},{225,... | collective-permute-start | bytes 786440 | tf_op jit(solution)/shard_map/ppermute | solution.py:313
  38.5 4.0 %collective-permute-start.7 = (bf16[128,256]{1,0:T(8,128)(2,1)S(1)}, bf16[128,256]{1,0:T(8,128)(2,1)S(1)}, u32[]{:S(2)}, u32[]{:S(2)}) collective-permute-start(bf16[128,256]{1,0:T(8,128)(2,1)S(1)} %get-tuple-element.14), channel_id=1, source_target_pairs={{0,28},{4,0},{8,4},{12,8},{16,12},{20,16},{24,20},{28,24},{1,29},{... | collective-permute-start | bytes 196616 | tf_op jit(solution)/shard_map/ppermute | solution.py:309
  41.2 0.7 copy-start.2
  68.5 45.0 %collective-permute-start.9 = (bf16[128,256]{1,0:T(8,128)(2,1)S(1)}, bf16[128,256]{1,0:T(8,128)(2,1)S(1)}, u32[]{:S(2)}, u32[]{:S(2)}) collective-permute-start(bf16[128,256]{1,0:T(8,128)(2,1)S(1)} %get-tuple-element.11), channel_id=1, source_target_pairs={{0,224},{1,225},{2,226},{3,227},{4,228},{5,229},{6,230},{7,231},{8... | collective-permute-start | bytes 196616 | tf_op jit(solution)/shard_map/ppermute | solution.py:348
  69.8 95.9 %collective-permute-start.10 = (bf16[128,256]{1,0:T(8,128)(2,1)S(1)}, bf16[128,256]{1,0:T(8,128)(2,1)S(1)}, u32[]{:S(2)}, u32[]{:S(2)}) collective-permute-start(bf16[128,256]{1,0:T(8,128)(2,1)S(1)} %get-tuple-element.11), channel_id=1, source_target_pairs={{0,192},{1,193},{2,194},{3,195},{4,196},{5,197},{6,198},{7,199},{8... | collective-permute-start | bytes 196616 | tf_op jit(solution)/shard_map/ppermute | solution.py:348
  71.1 95.9 %collective-permute-start.11 = (bf16[128,256]{1,0:T(8,128)(2,1)S(1)}, bf16[128,256]{1,0:T(8,128)(2,1)S(1)}, u32[]{:S(2)}, u32[]{:S(2)}) collective-permute-start(bf16[128,256]{1,0:T(8,128)(2,1)S(1)} %get-tuple-element.11), channel_id=1, source_target_pairs={{0,160},{1,161},{2,162},{3,163},{4,164},{5,165},{6,166},{7,167},{8... | collective-permute-start | bytes 196616 | tf_op jit(solution)/shard_map/ppermute | solution.py:348
  105.9 87.6 %collective-permute-start.13 = (bf16[272,512]{1,0:T(8,128)(2,1)S(1)}, bf16[272,512]{1,0:T(8,128)(2,1)S(1)}, u32[]{:S(2)}, u32[]{:S(2)}) collective-permute-start(bf16[272,512]{1,0:T(8,128)(2,1)S(1)} %attend_1.1), channel_id=1, source_target_pairs={{0,32},{32,64},{64,96},{96,128},{128,160},{160,192},{192,224},{1,3... | collective-permute-start | bytes 835592 | tf_op jit(solution)/shard_map/ppermute | solution.py:313
  109.8 83.8 %collective-permute-start.14 = (bf16[272,512]{1,0:T(8,128)(2,1)S(1)}, bf16[272,512]{1,0:T(8,128)(2,1)S(1)}, u32[]{:S(2)}, u32[]{:S(2)}) collective-permute-start(bf16[272,512]{1,0:T(8,128)(2,1)S(1)} %attend_2.1), channel_id=1, source_target_pairs={{0,64},{32,96},{64,128},{96,160},{128,192},{160,224},{1,65},{33,97... | collective-permute-start | bytes 835592 | tf_op jit(solution)/shard_map/ppermute | solution.py:313
  113.5 80.1 %collective-permute-start.16 = (bf16[272,512]{1,0:T(8,128)(2,1)S(1)}, bf16[272,512]{1,0:T(8,128)(2,1)S(1)}, u32[]{:S(2)}, u32[]{:S(2)}) collective-permute-start(bf16[272,512]{1,0:T(8,128)(2,1)S(1)} %attend_3.1), channel_id=1, source_target_pairs={{0,96},{32,128},{64,160},{96,192},{128,224},{1,97},{33,129},{65,16... | collective-permute-start | bytes 835592 | tf_op jit(solution)/shard_map/ppermute | solution.py:313
  165.7 27.9 %collective-permute-start.18 = (bf16[272,512]{1,0:T(8,128)(2,1)S(1)}, bf16[272,512]{1,0:T(8,128)(2,1)S(1)}, u32[]{:S(2)}, u32[]{:S(2)}) collective-permute-start(bf16[272,512]{1,0:T(8,128)(2,1)S(1)} %attend_4.1), channel_id=1, source_target_pairs={{0,128},{32,160},{64,192},{96,224},{1,129},{33,161},{65,193},{97,2... | collective-permute-start | bytes 835592 | tf_op jit(solution)/shard_map/ppermute | solution.py:313
where the time goes:
time: 207 us; the launch traced here: 211 us
  starting transfers between devices  86.4 us (42%)
  Pallas kernels  84.8 us (41%)
  blocking collectives  28.6 us (14%)
  waiting for transfers between devices  8.05 us (4%)
  local copies, waits for them, and re-layouts  2.45 us (1%)
    pallas_call x5, Pallas kernels, attend_call(): pl.pallas_call(functools.partial(attend, d), name=f'attend_{d}', out_shap...  82.2 us
    ppermute x8, starting transfers between devices, to_group(): lax.ppermute(x, GROUP, [(i, i + step) for i in range(N_GROUPS) if 0 <= i...  61.5 us
    all_to_all x1, blocking collectives, shards(): return lax.all_to_all(out, 'kvh', split_axis=0, concat_axis=1, tiled=True)  15.1 us
    ppermute x8, starting transfers between devices, along_ring(): lax.ppermute(x, RING, [(i, (i + step) % N_RING) for i in range(N_RING)])  13.8 us
    all_to_all x1, blocking collectives, shards(): lax.all_to_all(by_head.reshape(rows, -1), 'kvh', split_axis=1, concat_axi...  13.5 us
    ppermute x3, starting transfers between devices, shards(): sink = jnp.where(g == far, lax.ppermute(first, GROUP, [(0, far)]), sink)  11.2 us
    ppermute x8, waiting for transfers between devices, along_ring(): lax.ppermute(x, RING, [(i, (i + step) % N_RING) for i in range(N_RING)])  8.02 us
  transfers between devices with their start and end apart: 19, of which 4 were waited for; matrix products, arithmetic and copies ran while one was open for 0% of the time, Pallas kernels for 40%

commit v1 on v0

--- a/solution.py
+++ b/solution.py
@@ -50,16 +50,14 @@
 
 
 def assemble(meta_ref, *refs):
-    blocks, (k_ref, v_ref) = refs[:9], refs[9:]
+    blocks, (k_ref, v_ref) = refs[:8], refs[8:]
     g, z = meta_ref[0], meta_ref[1]
     first, end = document_bounds(meta_ref)
-    half = BLOCK // 2
-    pieces = [(r, 0, ref) for ref, r in zip(blocks[:7], (0, 1, 7, 2, 6, 3, 5))]
-    pieces += [(4, 0, blocks[7]), (4, half, blocks[8])]
-    for r, offset, ref in pieces:
+    pieces = list(zip((0, 1, 7, 2, 6, 3, 5, 4), blocks))
+    for r, ref in pieces:
         n = ref.shape[0]
         block = lax.rem(z - r + N_RING, N_RING)
-        at = pl.multiple_of(block * BLOCK + offset, half)
+        at = pl.multiple_of(block * BLOCK, BLOCK)
         rows = pl.ds(at, n)
         pos = g * GROUP_KEYS + at + lax.broadcasted_iota(jnp.int32, (n, 1), 0)
         seen = ((pos >= first) & (pos < end)) | (pos < SINK)
@@ -328,11 +326,10 @@
     blocks, up, down = [kv], kv, kv
     for step in range(3):
         up, down = along_ring(up, 1), along_ring(down, -1)
-        visiting[REACH - step] = to_group(q, step - REACH)
         blocks += [up, down]
-    blocks += [along_ring(up[:half], 1), along_ring(down[half:], -1)]
-    visiting[1] = to_group(q, -1)
-
+    blocks.append(along_ring(up, 1))
+    for d in range(1, REACH + 1):
+        visiting[d] = to_group(q, -d)
     k, v = assemble_call(meta, blocks)
     parts = {}
     first = blocks[0][:half]

time: 207 us -> 199 us (0.961); the launches traced: 211 us -> 198 us
  starting transfers between devices: 86.4 us -> 31.2 us
  Pallas kernels: 84.8 us -> 130 us
    ppermute x8, starting transfers between devices: 61.5 us -> 16.2 us  [to_group(): lax.ppermute(x, GROUP, [(i, i + step) for i in range(N_GROUPS) if 0 <= i...]
    pallas_call x5, Pallas kernels: 82.2 us -> 127 us  [attend_call(): pl.pallas_call(functools.partial(attend, d), name=f'attend_{d}', out_shap...]
    ppermute x3, starting transfers between devices: 11.2 us -> 3.88 us  [shards(): sink = jnp.where(g == far, lax.ppermute(first, GROUP, [(0, far)]), sink)]
    ppermute x8 -> x7, starting transfers between devices: 13.8 us -> 11.1 us  [along_ring(): lax.ppermute(x, RING, [(i, (i + step) % N_RING) for i in range(N_RING)])]
    ppermute x8 -> x7, waiting for transfers between devices: 8.02 us -> 6.7 us  [along_ring(): lax.ppermute(x, RING, [(i, (i + step) % N_RING) for i in range(N_RING)])]
  transfers between devices with their start and end apart: 19 -> 18, of which waited for: 4 -> 4; matrix products, arithmetic and copies ran while one was open for 0% -> 0% of each run, Pallas kernels for 40% -> 65%
where the time goes in v1:
time: 199 us; the launch traced here: 198 us
  Pallas kernels  130 us (65%)
  starting transfers between devices  31.2 us (16%)
  blocking collectives  27 us (14%)
  waiting for transfers between devices  6.73 us (3%)
  local copies, waits for them, and re-layouts  2.44 us (1%)
    pallas_call x5, Pallas kernels, attend_call(): pl.pallas_call(functools.partial(attend, d), name=f'attend_{d}', out_shap...  127 us
    ppermute x8, starting transfers between devices, to_group(): lax.ppermute(x, GROUP, [(i, i + step) for i in range(N_GROUPS) if 0 <= i...  16.2 us
    all_to_all x1, blocking collectives, shards(): lax.all_to_all(by_head.reshape(rows, -1), 'kvh', split_axis=1, concat_axi...  13.5 us
    all_to_all x1, blocking collectives, shards(): return lax.all_to_all(out, 'kvh', split_axis=0, concat_axis=1, tiled=True)  13.5 us
    ppermute x7, starting transfers between devices, along_ring(): lax.ppermute(x, RING, [(i, (i + step) % N_RING) for i in range(N_RING)])  11.1 us
    ppermute x7, waiting for transfers between devices, along_ring(): lax.ppermute(x, RING, [(i, (i + step) % N_RING) for i in range(N_RING)])  6.7 us
  transfers between devices with their start and end apart: 18, of which 4 were waited for; matrix products, arithmetic and copies ran while one was open for 0% of the time, Pallas kernels for 65%

profile of v1, /device:TPU:1, one launch (start us, length us, event | category | flops | bytes accessed | tf_op | source)
XLA Modules:
  0.0 197.8 jit_solution(4316485969899815299)
XLA Ops:
  1.1 13.5 %all_to_all.35 = bf16[64,4,768]{2,0,1:T(8,128)(2,1)S(1)} all-to-all(bf16[64,4,768]{2,0,1:T(8,128)(2,1)S(1)} %pad_maximum_fusion), channel_id=1, replica_groups=mesh['ctx_0'=2,'ctx_1'=4,'ctx_2'=8,'kvh'=4] {'kvh'}, dimensions={1} | all-to-all | bytes 786432 | tf_op jit(solution)/shard_map/all_to_all | solution.py:318
  14.7 1.7 collective-permute-start
  16.3 4.0 %collective-permute-start.1 = (bf16[256,256]{1,0:T(8,128)(2,1)S(1)}, bf16[256,256]{1,0:T(8,128)(2,1)S(1)}, u32[]{:S(2)}, u32[]{:S(2)}) collective-permute-start(bf16[256,256]{1,0:T(8,128)(2,1)S(1)} %slice.42.refs_0_), channel_id=1, source_target_pairs={{0,28},{4,0},{8,4},{12,8},{16,12},{20,16},{24,20},{28,24},{1,29},{... | collective-permute-start | bytes 393224 | tf_op jit(solution)/shard_map/ppermute | solution.py:307
  20.4 2.7 %collective-permute-done.refs_1_ = bf16[256,256]{1,0:T(8,128)(2,1)S(1)} collective-permute-done((bf16[256,256]{1,0:T(8,128)(2,1)S(1)}, bf16[256,256]{1,0:T(8,128)(2,1)S(1)}, u32[]{:S(2)}, u32[]{:S(2)}) %collective-permute-start) | collective-permute-done | bytes 131104 | tf_op jit(solution)/shard_map/ppermute | solution.py:307
  23.1 2.7 %collective-permute-start.3 = (bf16[256,256]{1,0:T(8,128)(2,1)S(1)}, bf16[256,256]{1,0:T(8,128)(2,1)S(1)}, u32[]{:S(2)}, u32[]{:S(2)}) collective-permute-start(bf16[256,256]{1,0:T(8,128)(2,1)S(1)} %collective-permute-done.1.refs_2_), channel_id=1, source_target_pairs={{0,28},{4,0},{8,4},{12,8},{16,12},{20,16},{24,20},{28,24},{1,29},{... | collective-permute-start | bytes 393224 | tf_op jit(solution)/shard_map/ppermute | solution.py:307
  25.8 2.3 %collective-permute-done.2.refs_3_ = bf16[256,256]{1,0:T(8,128)(2,1)S(1)} collective-permute-done((bf16[256,256]{1,0:T(8,128)(2,1)S(1)}, bf16[256,256]{1,0:T(8,128)(2,1)S(1)}, u32[]{:S(2)}, u32[]{:S(2)}) %collective-permute-start.2) | collective-permute-done | bytes 131104 | tf_op jit(solution)/shard_map/ppermute | solution.py:307
  28.1 1.3 collective-permute-start.7
  29.4 2.7 %collective-permute-start.5 = (bf16[256,256]{1,0:T(8,128)(2,1)S(1)}, bf16[256,256]{1,0:T(8,128)(2,1)S(1)}, u32[]{:S(2)}, u32[]{:S(2)}) collective-permute-start(bf16[256,256]{1,0:T(8,128)(2,1)S(1)} %collective-permute-done.3.refs_4_), channel_id=1, source_target_pairs={{0,28},{4,0},{8,4},{12,8},{16,12},{20,16},{24,20},{28,24},{1,29},{... | collective-permute-start | bytes 393224 | tf_op jit(solution)/shard_map/ppermute | solution.py:307
  35.2 1.3 collective-permute-start.14
  36.5 1.3 collective-permute-start.16
  39.6 24.8 %attend_2.1 = bf16[272,512]{1,0:T(8,128)(2,1)S(1)} custom-call(s32[18]{0:T(128)S(1)} %pad_add_fusion.meta_ref, bf16[256,512]{1,0:T(8,128)(2,1)S(1)} %collective-permute-done.7.q_ref, bf16[2048,256]{1,0:T(8,128)(2,1)S(1)} %get-tuple-element.9.k_ref, bf16[2048,256]{1,0:T(8,128)(2,1)S(1)} %get-tuple-element.10.v_ref), custom_call_target="tpu_custom_call" | custom-call | flops 536870912 | bytes 3145728 | tf_op jit(solution)/shard_map/attend_2/pallas_call | solution.py:278
  64.5 1.3 collective-permute-start.8
  65.8 1.3 collective-permute-start.9
  67.1 1.3 collective-permute-start.10
  68.4 26.2 %attend_1.1 = bf16[272,512]{1,0:T(8,128)(2,1)S(1)} custom-call(s32[18]{0:T(128)S(1)} %pad_add_fusion.meta_ref, bf16[256,512]{1,0:T(8,128)(2,1)S(1)} %collective-permute-done.11.q_ref, bf16[2048,256]{1,0:T(8,128)(2,1)S(1)} %get-tuple-element.9.k_ref, bf16[2048,256]{1,0:T(8,128)(2,1)S(1)} %get-tuple-element.10.v_ref), custom_call_target="tpu_custom_call" | custom-call | flops 536870912 | bytes 3145728 | tf_op jit(solution)/shard_map/attend_1/pallas_call | solution.py:278
  94.6 1.3 collective-permute-start.12
  95.9 25.0 %attend_3.1 = bf16[272,512]{1,0:T(8,128)(2,1)S(1)} custom-call(s32[18]{0:T(128)S(1)} %pad_add_fusion.meta_ref, bf16[256,512]{1,0:T(8,128)(2,1)S(1)} %collective-permute-done.14.q_ref, bf16[2048,256]{1,0:T(8,128)(2,1)S(1)} %get-tuple-element.9.k_ref, bf16[2048,256]{1,0:T(8,128)(2,1)S(1)} %get-tuple-element.10.v_ref), custom_call_target="tpu_custom_call" | custom-call | flops 536870912 | bytes 3145728 | tf_op jit(solution)/shard_map/attend_3/pallas_call | solution.py:278
  120.9 7.1 %collective-permute-start.13 = (bf16[272,512]{1,0:T(8,128)(2,1)S(1)}, bf16[272,512]{1,0:T(8,128)(2,1)S(1)}, u32[]{:S(2)}, u32[]{:S(2)}) collective-permute-start(bf16[272,512]{1,0:T(8,128)(2,1)S(1)} %attend_2.1), channel_id=1, source_target_pairs={{0,64},{32,96},{64,128},{96,160},{128,192},{160,224},{1,65},{33,97... | collective-permute-start | bytes 835592 | tf_op jit(solution)/shard_map/ppermute | solution.py:311
  128.1 24.8 %attend_4.1 = bf16[272,512]{1,0:T(8,128)(2,1)S(1)} custom-call(s32[18]{0:T(128)S(1)} %pad_add_fusion.meta_ref, bf16[256,512]{1,0:T(8,128)(2,1)S(1)} %collective-permute-done.16.q_ref, bf16[2048,256]{1,0:T(8,128)(2,1)S(1)} %get-tuple-element.9.k_ref, bf16[2048,256]{1,0:T(8,128)(2,1)S(1)} %get-tuple-element.10.v_ref), custom_call_target="tpu_custom_call" | custom-call | flops 536870912 | bytes 3145728 | tf_op jit(solution)/shard_map/attend_4/pallas_call | solution.py:278
  152.9 1.3 collective-permute-start.15
  154.2 1.3 collective-permute-start.17
  155.6 26.5 %attend_0.1.own_ref = f32[272,512]{1,0:T(8,128)S(1)} custom-call(s32[18]{0:T(128)S(1)} %pad_add_fusion.meta_ref, bf16[256,512]{1,0:T(8,128)(2,1)S(1)} %slice.41.q_ref, bf16[2048,256]{1,0:T(8,128)(2,1)S(1)} %get-tuple-element.9.k_ref, bf16[2048,256]{1,0:T(8,128)(2,1)S(1)} %get-tuple-element.10.v_ref, bf16[128,256]{1,0:T(8,128)(2,1)S(1)} %select_select_fusion.refs_0_), custom_call_target="tpu_custom_call" | custom-call | flops 536870912 | bytes 3145728 | tf_op jit(solution)/shard_map/attend_0/pallas_call | solution.py:278
  182.1 1.5 merge.1
  183.6 13.5 %all_to_all.36 = bf16[4,64,512]{2,1,0:T(8,128)(2,1)S(1)} all-to-all(bf16[4,64,512]{2,1,0:T(8,128)(2,1)S(1)} %bitcast.23), channel_id=1, replica_groups=mesh['ctx_0'=2,'ctx_1'=4,'ctx_2'=8,'kvh'=4] {'kvh'}, dimensions={0} | all-to-all | bytes 524288 | tf_op jit(solution)/shard_map/all_to_all | solution.py:350
  (36 shorter events, 6.7 us)
Async XLA Ops:
  0.0 1.0 copy-start
  0.0 1.0 copy-start.1
  14.7 8.4 %collective-permute-start = (bf16[256,256]{1,0:T(8,128)(2,1)S(1)}, bf16[256,256]{1,0:T(8,128)(2,1)S(1)}, u32[]{:S(2)}, u32[]{:S(2)}) collective-permute-start(bf16[256,256]{1,0:T(8,128)(2,1)S(1)} %slice.42.refs_0_), channel_id=1, source_target_pairs={{0,4},{4,8},{8,12},{12,16},{16,20},{20,24},{24,28},{28,0},{1,5},{5... | collective-permute-start | bytes 393224 | tf_op jit(solution)/shard_map/ppermute | solution.py:307
  16.3 6.8 %collective-permute-start.1 = (bf16[256,256]{1,0:T(8,128)(2,1)S(1)}, bf16[256,256]{1,0:T(8,128)(2,1)S(1)}, u32[]{:S(2)}, u32[]{:S(2)}) collective-permute-start(bf16[256,256]{1,0:T(8,128)(2,1)S(1)} %slice.42.refs_0_), channel_id=1, source_target_pairs={{0,28},{4,0},{8,4},{12,8},{16,12},{20,16},{24,20},{28,24},{1,29},{... | collective-permute-start | bytes 393224 | tf_op jit(solution)/shard_map/ppermute | solution.py:307
  23.1 5.0 %collective-permute-start.2 = (bf16[256,256]{1,0:T(8,128)(2,1)S(1)}, bf16[256,256]{1,0:T(8,128)(2,1)S(1)}, u32[]{:S(2)}, u32[]{:S(2)}) collective-permute-start(bf16[256,256]{1,0:T(8,128)(2,1)S(1)} %collective-permute-done.refs_1_), channel_id=1, source_target_pairs={{0,4},{4,8},{8,12},{12,16},{16,20},{20,24},{24,28},{28,0},{1,5},{5... | collective-permute-start | bytes 393224 | tf_op jit(solution)/shard_map/ppermute | solution.py:307
  23.1 6.4 %collective-permute-start.3 = (bf16[256,256]{1,0:T(8,128)(2,1)S(1)}, bf16[256,256]{1,0:T(8,128)(2,1)S(1)}, u32[]{:S(2)}, u32[]{:S(2)}) collective-permute-start(bf16[256,256]{1,0:T(8,128)(2,1)S(1)} %collective-permute-done.1.refs_2_), channel_id=1, source_target_pairs={{0,28},{4,0},{8,4},{12,8},{16,12},{20,16},{24,20},{28,24},{1,29},{... | collective-permute-start | bytes 393224 | tf_op jit(solution)/shard_map/ppermute | solution.py:307
  28.1 5.0 %collective-permute-start.4 = (bf16[256,256]{1,0:T(8,128)(2,1)S(1)}, bf16[256,256]{1,0:T(8,128)(2,1)S(1)}, u32[]{:S(2)}, u32[]{:S(2)}) collective-permute-start(bf16[256,256]{1,0:T(8,128)(2,1)S(1)} %collective-permute-done.2.refs_3_), channel_id=1, source_target_pairs={{0,4},{4,8},{8,12},{12,16},{16,20},{20,24},{24,28},{28,0},{1,5},{5... | collective-permute-start | bytes 393224 | tf_op jit(solution)/shard_map/ppermute | solution.py:307
  28.1 11.5 %collective-permute-start.7 = (bf16[256,512]{1,0:T(8,128)(2,1)S(1)}, bf16[256,512]{1,0:T(8,128)(2,1)S(1)}, u32[]{:S(2)}, u32[]{:S(2)}) collective-permute-start(bf16[256,512]{1,0:T(8,128)(2,1)S(1)} %slice.41.q_ref), channel_id=1, source_target_pairs={{64,0},{96,32},{128,64},{160,96},{192,128},{224,160},{65,1},{97,33... | collective-permute-start | bytes 786440 | tf_op jit(solution)/shard_map/ppermute | solution.py:311
  29.4 7.0 %collective-permute-start.5 = (bf16[256,256]{1,0:T(8,128)(2,1)S(1)}, bf16[256,256]{1,0:T(8,128)(2,1)S(1)}, u32[]{:S(2)}, u32[]{:S(2)}) collective-permute-start(bf16[256,256]{1,0:T(8,128)(2,1)S(1)} %collective-permute-done.3.refs_4_), channel_id=1, source_target_pairs={{0,28},{4,0},{8,4},{12,8},{16,12},{20,16},{24,20},{28,24},{1,29},{... | collective-permute-start | bytes 393224 | tf_op jit(solution)/shard_map/ppermute | solution.py:307
  33.1 5.3 %collective-permute-start.6 = (bf16[256,256]{1,0:T(8,128)(2,1)S(1)}, bf16[256,256]{1,0:T(8,128)(2,1)S(1)}, u32[]{:S(2)}, u32[]{:S(2)}) collective-permute-start(bf16[256,256]{1,0:T(8,128)(2,1)S(1)} %collective-permute-done.4.refs_5_), channel_id=1, source_target_pairs={{0,4},{4,8},{8,12},{12,16},{16,20},{20,24},{24,28},{28,0},{1,5},{5... | collective-permute-start | bytes 393224 | tf_op jit(solution)/shard_map/ppermute | solution.py:307
  33.1 0.7 copy-start.2
  33.9 33.2 %collective-permute-start.11 = (bf16[256,512]{1,0:T(8,128)(2,1)S(1)}, bf16[256,512]{1,0:T(8,128)(2,1)S(1)}, u32[]{:S(2)}, u32[]{:S(2)}) collective-permute-start(bf16[256,512]{1,0:T(8,128)(2,1)S(1)} %slice.41.q_ref), channel_id=1, source_target_pairs={{32,0},{64,32},{96,64},{128,96},{160,128},{192,160},{224,192},{33,... | collective-permute-start | bytes 786440 | tf_op jit(solution)/shard_map/ppermute | solution.py:311
  35.2 59.4 %collective-permute-start.14 = (bf16[256,512]{1,0:T(8,128)(2,1)S(1)}, bf16[256,512]{1,0:T(8,128)(2,1)S(1)}, u32[]{:S(2)}, u32[]{:S(2)}) collective-permute-start(bf16[256,512]{1,0:T(8,128)(2,1)S(1)} %slice.41.q_ref), channel_id=1, source_target_pairs={{96,0},{128,32},{160,64},{192,96},{224,128},{97,1},{129,33},{161,6... | collective-permute-start | bytes 786440 | tf_op jit(solution)/shard_map/ppermute | solution.py:311
  36.5 84.5 %collective-permute-start.16 = (bf16[256,512]{1,0:T(8,128)(2,1)S(1)}, bf16[256,512]{1,0:T(8,128)(2,1)S(1)}, u32[]{:S(2)}, u32[]{:S(2)}) collective-permute-start(bf16[256,512]{1,0:T(8,128)(2,1)S(1)} %slice.41.q_ref), channel_id=1, source_target_pairs={{128,0},{160,32},{192,64},{224,96},{129,1},{161,33},{193,65},{225,... | collective-permute-start | bytes 786440 | tf_op jit(solution)/shard_map/ppermute | solution.py:311
  64.5 88.4 %collective-permute-start.8 = (bf16[128,256]{1,0:T(8,128)(2,1)S(1)}, bf16[128,256]{1,0:T(8,128)(2,1)S(1)}, u32[]{:S(2)}, u32[]{:S(2)}) collective-permute-start(bf16[128,256]{1,0:T(8,128)(2,1)S(1)} %fusion.5), channel_id=1, source_target_pairs={{0,224},{1,225},{2,226},{3,227},{4,228},{5,229},{6,230},{7,231},{8... | collective-permute-start | bytes 196616 | tf_op jit(solution)/shard_map/ppermute | solution.py:345
  65.8 88.4 %collective-permute-start.9 = (bf16[128,256]{1,0:T(8,128)(2,1)S(1)}, bf16[128,256]{1,0:T(8,128)(2,1)S(1)}, u32[]{:S(2)}, u32[]{:S(2)}) collective-permute-start(bf16[128,256]{1,0:T(8,128)(2,1)S(1)} %fusion.5), channel_id=1, source_target_pairs={{0,192},{1,193},{2,194},{3,195},{4,196},{5,197},{6,198},{7,199},{8... | collective-permute-start | bytes 196616 | tf_op jit(solution)/shard_map/ppermute | solution.py:345
  67.1 88.4 %collective-permute-start.10 = (bf16[128,256]{1,0:T(8,128)(2,1)S(1)}, bf16[128,256]{1,0:T(8,128)(2,1)S(1)}, u32[]{:S(2)}, u32[]{:S(2)}) collective-permute-start(bf16[128,256]{1,0:T(8,128)(2,1)S(1)} %fusion.5), channel_id=1, source_target_pairs={{0,160},{1,161},{2,162},{3,163},{4,164},{5,165},{6,166},{7,167},{8... | collective-permute-start | bytes 196616 | tf_op jit(solution)/shard_map/ppermute | solution.py:345
  94.6 87.4 %collective-permute-start.12 = (bf16[272,512]{1,0:T(8,128)(2,1)S(1)}, bf16[272,512]{1,0:T(8,128)(2,1)S(1)}, u32[]{:S(2)}, u32[]{:S(2)}) collective-permute-start(bf16[272,512]{1,0:T(8,128)(2,1)S(1)} %attend_1.1), channel_id=1, source_target_pairs={{0,32},{32,64},{64,96},{96,128},{128,160},{160,192},{192,224},{1,3... | collective-permute-start | bytes 835592 | tf_op jit(solution)/shard_map/ppermute | solution.py:311
  120.9 61.1 %collective-permute-start.13 = (bf16[272,512]{1,0:T(8,128)(2,1)S(1)}, bf16[272,512]{1,0:T(8,128)(2,1)S(1)}, u32[]{:S(2)}, u32[]{:S(2)}) collective-permute-start(bf16[272,512]{1,0:T(8,128)(2,1)S(1)} %attend_2.1), channel_id=1, source_target_pairs={{0,64},{32,96},{64,128},{96,160},{128,192},{160,224},{1,65},{33,97... | collective-permute-start | bytes 835592 | tf_op jit(solution)/shard_map/ppermute | solution.py:311
  152.9 29.2 %collective-permute-start.15 = (bf16[272,512]{1,0:T(8,128)(2,1)S(1)}, bf16[272,512]{1,0:T(8,128)(2,1)S(1)}, u32[]{:S(2)}, u32[]{:S(2)}) collective-permute-start(bf16[272,512]{1,0:T(8,128)(2,1)S(1)} %attend_3.1), channel_id=1, source_target_pairs={{0,96},{32,128},{64,160},{96,192},{128,224},{1,97},{33,129},{65,16... | collective-permute-start | bytes 835592 | tf_op jit(solution)/shard_map/ppermute | solution.py:311
  154.2 27.8 %collective-permute-start.17 = (bf16[272,512]{1,0:T(8,128)(2,1)S(1)}, bf16[272,512]{1,0:T(8,128)(2,1)S(1)}, u32[]{:S(2)}, u32[]{:S(2)}) collective-permute-start(bf16[272,512]{1,0:T(8,128)(2,1)S(1)} %attend_4.1), channel_id=1, source_target_pairs={{0,128},{32,160},{64,192},{96,224},{1,129},{33,161},{65,193},{97,2... | collective-permute-start | bytes 835592 | tf_op jit(solution)/shard_map/ppermute | solution.py:311

commit v2 on v1

--- a/solution.py
+++ b/solution.py
@@ -49,11 +49,11 @@
     return start
 
 
-def assemble(meta_ref, *refs):
-    blocks, (k_ref, v_ref) = refs[:8], refs[8:]
+def assemble(places, meta_ref, *refs):
+    blocks, (k_ref, v_ref) = refs[: len(places)], refs[-2:]
     g, z = meta_ref[0], meta_ref[1]
     first, end = document_bounds(meta_ref)
-    pieces = list(zip((0, 1, 7, 2, 6, 3, 5, 4), blocks))
+    pieces = list(zip(places, blocks))
     for r, ref in pieces:
         n = ref.shape[0]
         block = lax.rem(z - r + N_RING, N_RING)
@@ -257,16 +257,18 @@
 SMEM = pl.BlockSpec(memory_space=pltpu.SMEM)
 
 
-def assemble_call(meta, blocks):
+def assemble_call(meta, places, blocks, *held):
+    n = 1 + len(blocks)
     return pl.pallas_call(
-        assemble,
-        name="assemble",
+        functools.partial(assemble, places),
+        name=f"assemble_{len(places)}",
         out_shape=[jax.ShapeDtypeStruct((GROUP_KEYS, 2 * HEAD), jnp.bfloat16)] * 2,
-        in_specs=[SMEM] + [VMEM] * len(blocks),
+        in_specs=[SMEM] + [VMEM] * (len(blocks) + len(held)),
         out_specs=[VMEM, VMEM],
+        input_output_aliases={n: 0, n + 1: 1} if held else {},
         compiler_params=pltpu.CompilerParams(vmem_limit_bytes=12 << 20),
         cost_estimate=pl.CostEstimate(flops=1 << 20, transcendentals=0, bytes_accessed=3 << 20),
-    )(meta, *blocks)
+    )(meta, *blocks, *held)
 
 
 def cost(width):
@@ -330,7 +332,8 @@
     blocks.append(along_ring(up, 1))
     for d in range(1, REACH + 1):
         visiting[d] = to_group(q, -d)
-    k, v = assemble_call(meta, blocks)
+    held = assemble_call(meta, (0, 1, 7, 2, 6, 3), blocks[:6])
+    k, v = assemble_call(meta, (5, 4), blocks[6:], *held)
     parts = {}
     first = blocks[0][:half]
     for r, i in enumerate((1, 3, 5, 7, 6, 4, 2), 1):

time: 199 us -> 197 us (0.990); the launches traced: 198 us -> 199 us
  Pallas kernels: 130 us -> 108 us
  starting transfers between devices: 31.2 us -> 52.1 us
  blocking collectives: 27 us -> 30.1 us
    pallas_call x5, Pallas kernels: 127 us -> 105 us  [attend_call(): pl.pallas_call(functools.partial(attend, d), name=f'attend_{d}', out_shap...]
    ppermute x8, starting transfers between devices: 16.2 us -> 28.9 us  [to_group(): lax.ppermute(x, GROUP, [(i, i + step) for i in range(N_GROUPS) if 0 <= i...]
    ppermute x3, starting transfers between devices: 3.88 us -> 12.1 us  [shards(): sink = jnp.where(g == far, lax.ppermute(first, GROUP, [(0, far)]), sink)]
    all_to_all x1, blocking collectives: 13.5 us -> 16.5 us  [shards(): return lax.all_to_all(out, 'kvh', split_axis=0, concat_axis=1, tiled=True)]
  transfers between devices with their start and end apart: 18 -> 18, of which waited for: 4 -> 3; matrix products, arithmetic and copies ran while one was open for 0% -> 0% of each run, Pallas kernels for 65% -> 53%
where the time goes in v2:
time: 197 us; the launch traced here: 199 us
  Pallas kernels  108 us (55%)
  starting transfers between devices  52.1 us (26%)
  blocking collectives  30.1 us (15%)
  waiting for transfers between devices  6.05 us (3%)
  local copies, waits for them, and re-layouts  2.44 us (1%)
    pallas_call x5, Pallas kernels, attend_call(): pl.pallas_call(functools.partial(attend, d), name=f'attend_{d}', out_shap...  105 us
    ppermute x8, starting transfers between devices, to_group(): lax.ppermute(x, GROUP, [(i, i + step) for i in range(N_GROUPS) if 0 <= i...  28.9 us
    all_to_all x1, blocking collectives, shards(): return lax.all_to_all(out, 'kvh', split_axis=0, concat_axis=1, tiled=True)  16.5 us
    all_to_all x1, blocking collectives, shards(): lax.all_to_all(by_head.reshape(rows, -1), 'kvh', split_axis=1, concat_axi...  13.5 us
    ppermute x3, starting transfers between devices, shards(): sink = jnp.where(g == far, lax.ppermute(first, GROUP, [(0, far)]), sink)  12.1 us
    ppermute x7, starting transfers between devices, along_ring(): lax.ppermute(x, RING, [(i, (i + step) % N_RING) for i in range(N_RING)])  11.1 us
    ppermute x7, waiting for transfers between devices, along_ring(): lax.ppermute(x, RING, [(i, (i + step) % N_RING) for i in range(N_RING)])  6.02 us
  transfers between devices with their start and end apart: 18, of which 3 were waited for; matrix products, arithmetic and copies ran while one was open for 0% of the time, Pallas kernels for 53%

profile of v2, /device:TPU:1, one launch (start us, length us, event | category | flops | bytes accessed | tf_op | source)
XLA Modules:
  0.0 199.1 jit_solution(13461359857479655204)
XLA Ops:
  1.1 13.5 %all_to_all.35 = bf16[64,4,768]{2,0,1:T(8,128)(2,1)S(1)} all-to-all(bf16[64,4,768]{2,0,1:T(8,128)(2,1)S(1)} %pad_maximum_fusion), channel_id=1, replica_groups=mesh['ctx_0'=2,'ctx_1'=4,'ctx_2'=8,'kvh'=4] {'kvh'}, dimensions={1} | all-to-all | bytes 786432 | tf_op jit(solution)/shard_map/all_to_all | solution.py:320
  14.7 1.7 collective-permute-start.3
  16.3 4.0 %collective-permute-start = (bf16[256,256]{1,0:T(8,128)(2,1)S(1)}, bf16[256,256]{1,0:T(8,128)(2,1)S(1)}, u32[]{:S(2)}, u32[]{:S(2)}) collective-permute-start(bf16[256,256]{1,0:T(8,128)(2,1)S(1)} %slice.42.refs_0_), channel_id=1, source_target_pairs={{0,28},{4,0},{8,4},{12,8},{16,12},{20,16},{24,20},{28,24},{1,29},{... | collective-permute-start | bytes 393224 | tf_op jit(solution)/shard_map/ppermute | solution.py:309
  20.4 2.7 %collective-permute-done.3.refs_1_ = bf16[256,256]{1,0:T(8,128)(2,1)S(1)} collective-permute-done((bf16[256,256]{1,0:T(8,128)(2,1)S(1)}, bf16[256,256]{1,0:T(8,128)(2,1)S(1)}, u32[]{:S(2)}, u32[]{:S(2)}) %collective-permute-start.3) | collective-permute-done | bytes 131104 | tf_op jit(solution)/shard_map/ppermute | solution.py:309
  23.1 2.7 %collective-permute-start.1 = (bf16[256,256]{1,0:T(8,128)(2,1)S(1)}, bf16[256,256]{1,0:T(8,128)(2,1)S(1)}, u32[]{:S(2)}, u32[]{:S(2)}) collective-permute-start(bf16[256,256]{1,0:T(8,128)(2,1)S(1)} %collective-permute-done.refs_2_), channel_id=1, source_target_pairs={{0,28},{4,0},{8,4},{12,8},{16,12},{20,16},{24,20},{28,24},{1,29},{... | collective-permute-start | bytes 393224 | tf_op jit(solution)/shard_map/ppermute | solution.py:309
  25.8 2.3 %collective-permute-done.4.refs_3_ = bf16[256,256]{1,0:T(8,128)(2,1)S(1)} collective-permute-done((bf16[256,256]{1,0:T(8,128)(2,1)S(1)}, bf16[256,256]{1,0:T(8,128)(2,1)S(1)}, u32[]{:S(2)}, u32[]{:S(2)}) %collective-permute-start.4) | collective-permute-done | bytes 131104 | tf_op jit(solution)/shard_map/ppermute | solution.py:309
  28.1 1.3 collective-permute-start.7
  29.4 2.7 %collective-permute-start.2 = (bf16[256,256]{1,0:T(8,128)(2,1)S(1)}, bf16[256,256]{1,0:T(8,128)(2,1)S(1)}, u32[]{:S(2)}, u32[]{:S(2)}) collective-permute-start(bf16[256,256]{1,0:T(8,128)(2,1)S(1)} %collective-permute-done.1.refs_4_), channel_id=1, source_target_pairs={{0,28},{4,0},{8,4},{12,8},{16,12},{20,16},{24,20},{28,24},{1,29},{... | collective-permute-start | bytes 393224 | tf_op jit(solution)/shard_map/ppermute | solution.py:309
  35.2 1.3 collective-permute-start.14
  37.5 1.3 collective-permute-start.11
  39.5 24.8 %attend_2.1 = bf16[272,512]{1,0:T(8,128)(2,1)S(1)} custom-call(s32[18]{0:T(128)S(1)} %pad_add_fusion.meta_ref, bf16[256,512]{1,0:T(8,128)(2,1)S(1)} %collective-permute-done.7.q_ref, bf16[2048,256]{1,0:T(8,128)(2,1)S(1)} %get-tuple-element.13.k_ref, bf16[2048,256]{1,0:T(8,128)(2,1)S(1)} %get-tuple-element.14.v_ref), custom_call_target="tpu_custom_call" | custom-call | flops 536870912 | bytes 3145728 | tf_op jit(solution)/shard_map/attend_2/pallas_call | solution.py:280
  64.3 9.5 %collective-permute-start.10 = (bf16[128,256]{1,0:T(8,128)(2,1)S(1)}, bf16[128,256]{1,0:T(8,128)(2,1)S(1)}, u32[]{:S(2)}, u32[]{:S(2)}) collective-permute-start(bf16[128,256]{1,0:T(8,128)(2,1)S(1)} %fusion.5), channel_id=1, source_target_pairs={{0,160},{1,161},{2,162},{3,163},{4,164},{5,165},{6,166},{7,167},{8... | collective-permute-start | bytes 196616 | tf_op jit(solution)/shard_map/ppermute | solution.py:348
  73.8 1.3 collective-permute-start.8
  75.1 1.3 collective-permute-start.9
  76.4 2.4 %attend_4.1 = bf16[272,512]{1,0:T(8,128)(2,1)S(1)} custom-call(s32[18]{0:T(128)S(1)} %pad_add_fusion.meta_ref, bf16[256,512]{1,0:T(8,128)(2,1)S(1)} %collective-permute-done.16.q_ref, bf16[2048,256]{1,0:T(8,128)(2,1)S(1)} %get-tuple-element.13.k_ref, bf16[2048,256]{1,0:T(8,128)(2,1)S(1)} %get-tuple-element.14.v_ref), custom_call_target="tpu_custom_call" | custom-call | flops 536870912 | bytes 3145728 | tf_op jit(solution)/shard_map/attend_4/pallas_call | solution.py:280
  78.8 1.3 collective-permute-start.17
  80.1 25.0 %attend_3.1 = bf16[272,512]{1,0:T(8,128)(2,1)S(1)} custom-call(s32[18]{0:T(128)S(1)} %pad_add_fusion.meta_ref, bf16[256,512]{1,0:T(8,128)(2,1)S(1)} %collective-permute-done.14.q_ref, bf16[2048,256]{1,0:T(8,128)(2,1)S(1)} %get-tuple-element.13.k_ref, bf16[2048,256]{1,0:T(8,128)(2,1)S(1)} %get-tuple-element.14.v_ref), custom_call_target="tpu_custom_call" | custom-call | flops 536870912 | bytes 3145728 | tf_op jit(solution)/shard_map/attend_3/pallas_call | solution.py:280
  105.1 18.8 %collective-permute-start.15 = (bf16[272,512]{1,0:T(8,128)(2,1)S(1)}, bf16[272,512]{1,0:T(8,128)(2,1)S(1)}, u32[]{:S(2)}, u32[]{:S(2)}) collective-permute-start(bf16[272,512]{1,0:T(8,128)(2,1)S(1)} %attend_3.1), channel_id=1, source_target_pairs={{0,96},{32,128},{64,160},{96,192},{128,224},{1,97},{33,129},{65,16... | collective-permute-start | bytes 835592 | tf_op jit(solution)/shard_map/ppermute | solution.py:313
  124.0 26.2 %attend_1.1 = bf16[272,512]{1,0:T(8,128)(2,1)S(1)} custom-call(s32[18]{0:T(128)S(1)} %pad_add_fusion.meta_ref, bf16[256,512]{1,0:T(8,128)(2,1)S(1)} %collective-permute-done.11.q_ref, bf16[2048,256]{1,0:T(8,128)(2,1)S(1)} %get-tuple-element.13.k_ref, bf16[2048,256]{1,0:T(8,128)(2,1)S(1)} %get-tuple-element.14.v_ref), custom_call_target="tpu_custom_call" | custom-call | flops 536870912 | bytes 3145728 | tf_op jit(solution)/shard_map/attend_1/pallas_call | solution.py:280
  150.2 1.3 collective-permute-start.12
  151.5 2.3 %collective-permute-start.13 = (bf16[272,512]{1,0:T(8,128)(2,1)S(1)}, bf16[272,512]{1,0:T(8,128)(2,1)S(1)}, u32[]{:S(2)}, u32[]{:S(2)}) collective-permute-start(bf16[272,512]{1,0:T(8,128)(2,1)S(1)} %attend_2.1), channel_id=1, source_target_pairs={{0,64},{32,96},{64,128},{96,160},{128,192},{160,224},{1,65},{33,97... | collective-permute-start | bytes 835592 | tf_op jit(solution)/shard_map/ppermute | solution.py:313
  153.8 26.5 %attend_0.1.own_ref = f32[272,512]{1,0:T(8,128)S(1)} custom-call(s32[18]{0:T(128)S(1)} %pad_add_fusion.meta_ref, bf16[256,512]{1,0:T(8,128)(2,1)S(1)} %slice.41.q_ref, bf16[2048,256]{1,0:T(8,128)(2,1)S(1)} %get-tuple-element.13.k_ref, bf16[2048,256]{1,0:T(8,128)(2,1)S(1)} %get-tuple-element.14.v_ref, bf16[128,256]{1,0:T(8,128)(2,1)S(1)} %select_select_fusion.refs_0_), custom_call_target="tpu_custom_call" | custom-call | flops 536870912 | bytes 3145728 | tf_op jit(solution)/shard_map/attend_0/pallas_call | solution.py:280
  180.3 1.5 merge.1
  181.8 16.5 %all_to_all.36 = bf16[4,64,512]{2,1,0:T(8,128)(2,1)S(1)} all-to-all(bf16[4,64,512]{2,1,0:T(8,128)(2,1)S(1)} %bitcast.23), channel_id=1, replica_groups=mesh['ctx_0'=2,'ctx_1'=4,'ctx_2'=8,'kvh'=4] {'kvh'}, dimensions={0} | all-to-all | bytes 524288 | tf_op jit(solution)/shard_map/all_to_all | solution.py:353
  (37 shorter events, 6.5 us)
Async XLA Ops:
  0.0 1.0 copy-start
  0.0 1.0 copy-start.1
  14.7 8.4 %collective-permute-start.3 = (bf16[256,256]{1,0:T(8,128)(2,1)S(1)}, bf16[256,256]{1,0:T(8,128)(2,1)S(1)}, u32[]{:S(2)}, u32[]{:S(2)}) collective-permute-start(bf16[256,256]{1,0:T(8,128)(2,1)S(1)} %slice.42.refs_0_), channel_id=1, source_target_pairs={{0,4},{4,8},{8,12},{12,16},{16,20},{20,24},{24,28},{28,0},{1,5},{5... | collective-permute-start | bytes 393224 | tf_op jit(solution)/shard_map/ppermute | solution.py:309
  16.3 6.8 %collective-permute-start = (bf16[256,256]{1,0:T(8,128)(2,1)S(1)}, bf16[256,256]{1,0:T(8,128)(2,1)S(1)}, u32[]{:S(2)}, u32[]{:S(2)}) collective-permute-start(bf16[256,256]{1,0:T(8,128)(2,1)S(1)} %slice.42.refs_0_), channel_id=1, source_target_pairs={{0,28},{4,0},{8,4},{12,8},{16,12},{20,16},{24,20},{28,24},{1,29},{... | collective-permute-start | bytes 393224 | tf_op jit(solution)/shard_map/ppermute | solution.py:309
  23.1 5.0 %collective-permute-start.4 = (bf16[256,256]{1,0:T(8,128)(2,1)S(1)}, bf16[256,256]{1,0:T(8,128)(2,1)S(1)}, u32[]{:S(2)}, u32[]{:S(2)}) collective-permute-start(bf16[256,256]{1,0:T(8,128)(2,1)S(1)} %collective-permute-done.3.refs_1_), channel_id=1, source_target_pairs={{0,4},{4,8},{8,12},{12,16},{16,20},{20,24},{24,28},{28,0},{1,5},{5... | collective-permute-start | bytes 393224 | tf_op jit(solution)/shard_map/ppermute | solution.py:309
  23.1 6.4 %collective-permute-start.1 = (bf16[256,256]{1,0:T(8,128)(2,1)S(1)}, bf16[256,256]{1,0:T(8,128)(2,1)S(1)}, u32[]{:S(2)}, u32[]{:S(2)}) collective-permute-start(bf16[256,256]{1,0:T(8,128)(2,1)S(1)} %collective-permute-done.refs_2_), channel_id=1, source_target_pairs={{0,28},{4,0},{8,4},{12,8},{16,12},{20,16},{24,20},{28,24},{1,29},{... | collective-permute-start | bytes 393224 | tf_op jit(solution)/shard_map/ppermute | solution.py:309
  28.1 5.0 %collective-permute-start.5 = (bf16[256,256]{1,0:T(8,128)(2,1)S(1)}, bf16[256,256]{1,0:T(8,128)(2,1)S(1)}, u32[]{:S(2)}, u32[]{:S(2)}) collective-permute-start(bf16[256,256]{1,0:T(8,128)(2,1)S(1)} %collective-permute-done.4.refs_3_), channel_id=1, source_target_pairs={{0,4},{4,8},{8,12},{12,16},{16,20},{20,24},{24,28},{28,0},{1,5},{5... | collective-permute-start | bytes 393224 | tf_op jit(solution)/shard_map/ppermute | solution.py:309
  28.1 11.3 %collective-permute-start.7 = (bf16[256,512]{1,0:T(8,128)(2,1)S(1)}, bf16[256,512]{1,0:T(8,128)(2,1)S(1)}, u32[]{:S(2)}, u32[]{:S(2)}) collective-permute-start(bf16[256,512]{1,0:T(8,128)(2,1)S(1)} %slice.41.q_ref), channel_id=1, source_target_pairs={{64,0},{96,32},{128,64},{160,96},{192,128},{224,160},{65,1},{97,33... | collective-permute-start | bytes 786440 | tf_op jit(solution)/shard_map/ppermute | solution.py:313
  29.4 8.0 %collective-permute-start.2 = (bf16[256,256]{1,0:T(8,128)(2,1)S(1)}, bf16[256,256]{1,0:T(8,128)(2,1)S(1)}, u32[]{:S(2)}, u32[]{:S(2)}) collective-permute-start(bf16[256,256]{1,0:T(8,128)(2,1)S(1)} %collective-permute-done.1.refs_4_), channel_id=1, source_target_pairs={{0,28},{4,0},{8,4},{12,8},{16,12},{20,16},{24,20},{28,24},{1,29},{... | collective-permute-start | bytes 393224 | tf_op jit(solution)/shard_map/ppermute | solution.py:309
  33.1 5.6 %collective-permute-start.6 = (bf16[256,256]{1,0:T(8,128)(2,1)S(1)}, bf16[256,256]{1,0:T(8,128)(2,1)S(1)}, u32[]{:S(2)}, u32[]{:S(2)}) collective-permute-start(bf16[256,256]{1,0:T(8,128)(2,1)S(1)} %collective-permute-done.5.refs_5_), channel_id=1, source_target_pairs={{0,4},{4,8},{8,12},{12,16},{16,20},{20,24},{24,28},{28,0},{1,5},{5... | collective-permute-start | bytes 393224 | tf_op jit(solution)/shard_map/ppermute | solution.py:309
  33.1 0.7 copy-start.2
  33.9 41.2 %collective-permute-start.16 = (bf16[256,512]{1,0:T(8,128)(2,1)S(1)}, bf16[256,512]{1,0:T(8,128)(2,1)S(1)}, u32[]{:S(2)}, u32[]{:S(2)}) collective-permute-start(bf16[256,512]{1,0:T(8,128)(2,1)S(1)} %slice.41.q_ref), channel_id=1, source_target_pairs={{128,0},{160,32},{192,64},{224,96},{129,1},{161,33},{193,65},{225,... | collective-permute-start | bytes 786440 | tf_op jit(solution)/shard_map/ppermute | solution.py:313
  35.2 43.6 %collective-permute-start.14 = (bf16[256,512]{1,0:T(8,128)(2,1)S(1)}, bf16[256,512]{1,0:T(8,128)(2,1)S(1)}, u32[]{:S(2)}, u32[]{:S(2)}) collective-permute-start(bf16[256,512]{1,0:T(8,128)(2,1)S(1)} %slice.41.q_ref), channel_id=1, source_target_pairs={{96,0},{128,32},{160,64},{192,96},{224,128},{97,1},{129,33},{161,6... | collective-permute-start | bytes 786440 | tf_op jit(solution)/shard_map/ppermute | solution.py:313
  37.5 67.7 %collective-permute-start.11 = (bf16[256,512]{1,0:T(8,128)(2,1)S(1)}, bf16[256,512]{1,0:T(8,128)(2,1)S(1)}, u32[]{:S(2)}, u32[]{:S(2)}) collective-permute-start(bf16[256,512]{1,0:T(8,128)(2,1)S(1)} %slice.41.q_ref), channel_id=1, source_target_pairs={{32,0},{64,32},{96,64},{128,96},{160,128},{192,160},{224,192},{33,... | collective-permute-start | bytes 786440 | tf_op jit(solution)/shard_map/ppermute | solution.py:313
  64.3 85.9 %collective-permute-start.10 = (bf16[128,256]{1,0:T(8,128)(2,1)S(1)}, bf16[128,256]{1,0:T(8,128)(2,1)S(1)}, u32[]{:S(2)}, u32[]{:S(2)}) collective-permute-start(bf16[128,256]{1,0:T(8,128)(2,1)S(1)} %fusion.5), channel_id=1, source_target_pairs={{0,160},{1,161},{2,162},{3,163},{4,164},{5,165},{6,166},{7,167},{8... | collective-permute-start | bytes 196616 | tf_op jit(solution)/shard_map/ppermute | solution.py:348
  73.8 77.7 %collective-permute-start.8 = (bf16[128,256]{1,0:T(8,128)(2,1)S(1)}, bf16[128,256]{1,0:T(8,128)(2,1)S(1)}, u32[]{:S(2)}, u32[]{:S(2)}) collective-permute-start(bf16[128,256]{1,0:T(8,128)(2,1)S(1)} %fusion.5), channel_id=1, source_target_pairs={{0,224},{1,225},{2,226},{3,227},{4,228},{5,229},{6,230},{7,231},{8... | collective-permute-start | bytes 196616 | tf_op jit(solution)/shard_map/ppermute | solution.py:348
  75.1 78.7 %collective-permute-start.9 = (bf16[128,256]{1,0:T(8,128)(2,1)S(1)}, bf16[128,256]{1,0:T(8,128)(2,1)S(1)}, u32[]{:S(2)}, u32[]{:S(2)}) collective-permute-start(bf16[128,256]{1,0:T(8,128)(2,1)S(1)} %fusion.5), channel_id=1, source_target_pairs={{0,192},{1,193},{2,194},{3,195},{4,196},{5,197},{6,198},{7,199},{8... | collective-permute-start | bytes 196616 | tf_op jit(solution)/shard_map/ppermute | solution.py:348
  78.8 101.5 %collective-permute-start.17 = (bf16[272,512]{1,0:T(8,128)(2,1)S(1)}, bf16[272,512]{1,0:T(8,128)(2,1)S(1)}, u32[]{:S(2)}, u32[]{:S(2)}) collective-permute-start(bf16[272,512]{1,0:T(8,128)(2,1)S(1)} %attend_4.1), channel_id=1, source_target_pairs={{0,128},{32,160},{64,192},{96,224},{1,129},{33,161},{65,193},{97,2... | collective-permute-start | bytes 835592 | tf_op jit(solution)/shard_map/ppermute | solution.py:313
  105.1 75.2 %collective-permute-start.15 = (bf16[272,512]{1,0:T(8,128)(2,1)S(1)}, bf16[272,512]{1,0:T(8,128)(2,1)S(1)}, u32[]{:S(2)}, u32[]{:S(2)}) collective-permute-start(bf16[272,512]{1,0:T(8,128)(2,1)S(1)} %attend_3.1), channel_id=1, source_target_pairs={{0,96},{32,128},{64,160},{96,192},{128,224},{1,97},{33,129},{65,16... | collective-permute-start | bytes 835592 | tf_op jit(solution)/shard_map/ppermute | solution.py:313
  150.2 30.1 %collective-permute-start.12 = (bf16[272,512]{1,0:T(8,128)(2,1)S(1)}, bf16[272,512]{1,0:T(8,128)(2,1)S(1)}, u32[]{:S(2)}, u32[]{:S(2)}) collective-permute-start(bf16[272,512]{1,0:T(8,128)(2,1)S(1)} %attend_1.1), channel_id=1, source_target_pairs={{0,32},{32,64},{64,96},{96,128},{128,160},{160,192},{192,224},{1,3... | collective-permute-start | bytes 835592 | tf_op jit(solution)/shard_map/ppermute | solution.py:313
  151.5 28.8 %collective-permute-start.13 = (bf16[272,512]{1,0:T(8,128)(2,1)S(1)}, bf16[272,512]{1,0:T(8,128)(2,1)S(1)}, u32[]{:S(2)}, u32[]{:S(2)}) collective-permute-start(bf16[272,512]{1,0:T(8,128)(2,1)S(1)} %attend_2.1), channel_id=1, source_target_pairs={{0,64},{32,96},{64,128},{96,160},{128,192},{160,224},{1,65},{33,97... | collective-permute-start | bytes 835592 | tf_op jit(solution)/shard_map/ppermute | solution.py:313
